TPU v7x, 32 devices: a whole 2x2x4 slice. The times are simulated.
32 devices in a mesh: tgt: 4 (over z), ptr: 8 (over y, x, core).
Axes of the slice: x: 2, y: 2, z: 4, core: 2. Of those that a mesh axis runs over, the one named last changes fastest.
Arguments:
- targets: float32 [32, 32, 1024], P('tgt'), may hold values from -12 to 12
- partners: float32 [32, 32, 1024], P(None, None, 'ptr'), may hold values from -6 to 6
- occupied: int32 [8], P('ptr'), may hold values 0 or 1
- retained: int32 [1], replicated, may hold values from 16 to 32
Outputs:
- compressed: float32 [32, 32, 1024], P('tgt', 'ptr')
All inputs are finite; a program needn't handle non-finite values. No bound on the sum of `occupied` on one device may be relied on, other than what follows from the above.
Results may differ from a plain program's by a relative error of at most 0.00008.
Values sent between devices are 32-bit elements; how exact they have to be, the bound alone decides.
A program may use at most 64 MiB of HBM per device.

v0:
```python
import math

import jax
import jax.numpy as jnp
from jax import lax
from jax.sharding import PartitionSpec as P

HIGHEST_PRECISION = lax.Precision.HIGHEST


def cas_matrix(length):
    indices = jnp.arange(length, dtype=jnp.int32)
    phases = (indices[:, None] * indices[None, :] % length).astype(jnp.float32) * (
        2.0 * math.pi / length
    )
    return jnp.cos(phases) + jnp.sin(phases)


def coulomb_table(length):
    indices = jnp.arange(length, dtype=jnp.int32)
    signed = jnp.where(indices < length // 2, indices, indices - length).astype(jnp.float32)
    wave = signed * (2.0 * math.pi / length)
    wave = wave * wave
    total = wave[:, None, None] + wave[None, :, None] + wave[None, None, :]
    safe = jnp.where(total > 0.0, total, jnp.float32(1.0))
    return jnp.where(total > 0.0, 4.0 * math.pi / safe, jnp.float32(0.0))


def transform(field, matrix, packed):
    length = matrix.shape[0]
    after_first = jnp.dot(matrix, field.reshape(length, -1), precision=HIGHEST_PRECISION)
    after_second = jnp.einsum(
        "ky,xyn->xkn", matrix, after_first.reshape(length, length, -1), precision=HIGHEST_PRECISION
    )
    after_third = jnp.dot(
        after_second.reshape(-1, packed.shape[0]), packed, precision=HIGHEST_PRECISION
    )
    return after_third.reshape(field.shape)


def shards(targets, partners, occupied, retained):
    length = targets.shape[1]
    owned_count = targets.shape[0]
    partner_count = partners.shape[2] // length
    plane_cells = length * length
    all_cells = plane_cells * length
    matrix = cas_matrix(length)
    packing = max(1, 128 // length)
    packed = jnp.kron(jnp.eye(packing, dtype=jnp.float32), matrix)
    kernel_wide = jnp.broadcast_to(
        (coulomb_table(length) / all_cells)[:, :, None, :], (length, length, partner_count, length)
    ).reshape(length, length, partner_count * length)
    occupancy = 0.25 + 0.75 * jnp.repeat(occupied.astype(jnp.float32), 4)
    weighted = (
        partners.reshape(length, length, partner_count, length) * occupancy[None, None, :, None]
    ).reshape(length, length, partner_count * length)

    def action(target_one):
        spread = jnp.broadcast_to(
            target_one.reshape(length, length, 1, length), (length, length, partner_count, length)
        ).reshape(length, length, partner_count * length)
        density = spread * partners
        potential = transform(kernel_wide * transform(density, matrix, packed), matrix, packed)
        summed = (weighted * potential).reshape(length, length, partner_count, length).sum(axis=2)
        return summed.reshape(length, plane_cells)

    slab_count = length // lax.axis_size("ptr")
    slab_start = lax.axis_index("ptr") * slab_count
    every_action = lax.map(action, targets)
    action_slab = lax.psum_scatter(every_action, "ptr", scatter_dimension=1, tiled=True)
    own_slab = lax.dynamic_slice_in_dim(targets, slab_start, slab_count, 1)
    target_slab = lax.all_gather(own_slab, "tgt", axis=0, tiled=True)
    total_targets = target_slab.shape[0]
    columns = (
        jnp.einsum("asm,bsm->ab", target_slab, action_slab, precision=HIGHEST_PRECISION) / all_cells
    )
    first_owned = lax.axis_index("tgt") * owned_count
    summed_columns = lax.psum(columns, "ptr")
    intersection = lax.all_gather(summed_columns, "tgt", axis=1, tiled=True)
    lower = jnp.linalg.cholesky(intersection)
    inverse = jax.scipy.linalg.solve_triangular(
        lower, jnp.eye(total_targets, dtype=jnp.float32), lower=True
    )
    all_actions = lax.all_gather(action_slab, "tgt", axis=0, tiled=True)
    own_rows = lax.dynamic_slice_in_dim(inverse, first_owned, owned_count, 0)
    result = jnp.einsum("bc,csm->bsm", own_rows, all_actions, precision=HIGHEST_PRECISION)
    global_rows = first_owned + jnp.arange(owned_count, dtype=jnp.int32)
    keeping = (global_rows < retained[0]).astype(jnp.float32)
    return result * keeping[:, None, None]


def solution(mesh):
    return jax.shard_map(
        shards,
        mesh=mesh,
        in_specs=(P("tgt", None, None), P(None, None, "ptr"), P("ptr"), P()),
        out_specs=P("tgt", "ptr", None),
        check_vma=False,
    )
```

profile of v0, /device:TPU:0, one launch (start us, length us, event | category | flops | bytes accessed | tf_op | source)
XLA Modules:
  0.0 249.2 jit_solution(11389717281387378908)
XLA Ops:
  10.3 142.0 %while.12 = (s32[]{:T(128)}, f32[8,32,1024]{2,0,1:T(8,128)}, f32[8,32,1024]{2,1,0:T(8,128)}, f32[32,32,128]{2,1,0:T(8,128)}, f32[32,32,128]{2,1,0:T(8,128)}, /*i...) while((s32[]{:T(128)}, f32[8,32,1024]{2,0,1:T(8,128)}, ...), condition=%wide.region_2.3_spmd.clone.clone, body=%wide.region_0.2_spmd.clone.clone.sunk | while | flops 604549120 | bytes 18551004 | solution.py:69
  14.1 1.9 reshape.200
  16.0 2.0 convolution_bitcast_fusion.9
  24.4 3.6 %dynamic_update_slice.7 = f32[8,32,1024]{2,0,1:T(8,128)} dynamic-update-slice(f32[8,32,1024]{2,0,1:T(8,128)} %get-tuple-element.185, f32[1,32,1024]{2,0,1:T(1,128)S(1)} %broadcast_in_dim.61, s32[]{:T(128)S(6)} %copy.36, s32[]{:T(128)} %constant.91.clone.1..sunk, s32[]{:T(128)} %constant.91.clone.1..sunk) | dynamic-update-slice | bytes 262148 | tf_op jit(solution)/shard_map/while/body/jit(dynamic_update_index_in_dim)/dynamic_update_slice | solution.py:69
  31.8 1.9 reshape.200
  33.7 2.0 convolution_bitcast_fusion.9
  42.2 3.6 %dynamic_update_slice.7 = f32[8,32,1024]{2,0,1:T(8,128)} dynamic-update-slice(f32[8,32,1024]{2,0,1:T(8,128)} %get-tuple-element.185, f32[1,32,1024]{2,0,1:T(1,128)S(1)} %broadcast_in_dim.61, s32[]{:T(128)S(6)} %copy.36, s32[]{:T(128)} %constant.91.clone.1..sunk, s32[]{:T(128)} %constant.91.clone.1..sunk) | dynamic-update-slice | bytes 262148 | tf_op jit(solution)/shard_map/while/body/jit(dynamic_update_index_in_dim)/dynamic_update_slice | solution.py:69
  49.6 1.9 reshape.200
  51.5 2.0 convolution_bitcast_fusion.9
  59.9 3.6 %dynamic_update_slice.7 = f32[8,32,1024]{2,0,1:T(8,128)} dynamic-update-slice(f32[8,32,1024]{2,0,1:T(8,128)} %get-tuple-element.185, f32[1,32,1024]{2,0,1:T(1,128)S(1)} %broadcast_in_dim.61, s32[]{:T(128)S(6)} %copy.36, s32[]{:T(128)} %constant.91.clone.1..sunk, s32[]{:T(128)} %constant.91.clone.1..sunk) | dynamic-update-slice | bytes 262148 | tf_op jit(solution)/shard_map/while/body/jit(dynamic_update_index_in_dim)/dynamic_update_slice | solution.py:69
  67.3 1.9 reshape.200
  69.2 2.0 convolution_bitcast_fusion.9
  77.7 3.6 %dynamic_update_slice.7 = f32[8,32,1024]{2,0,1:T(8,128)} dynamic-update-slice(f32[8,32,1024]{2,0,1:T(8,128)} %get-tuple-element.185, f32[1,32,1024]{2,0,1:T(1,128)S(1)} %broadcast_in_dim.61, s32[]{:T(128)S(6)} %copy.36, s32[]{:T(128)} %constant.91.clone.1..sunk, s32[]{:T(128)} %constant.91.clone.1..sunk) | dynamic-update-slice | bytes 262148 | tf_op jit(solution)/shard_map/while/body/jit(dynamic_update_index_in_dim)/dynamic_update_slice | solution.py:69
  85.1 1.9 reshape.200
  87.0 2.0 convolution_bitcast_fusion.9
  95.4 3.6 %dynamic_update_slice.7 = f32[8,32,1024]{2,0,1:T(8,128)} dynamic-update-slice(f32[8,32,1024]{2,0,1:T(8,128)} %get-tuple-element.185, f32[1,32,1024]{2,0,1:T(1,128)S(1)} %broadcast_in_dim.61, s32[]{:T(128)S(6)} %copy.36, s32[]{:T(128)} %constant.91.clone.1..sunk, s32[]{:T(128)} %constant.91.clone.1..sunk) | dynamic-update-slice | bytes 262148 | tf_op jit(solution)/shard_map/while/body/jit(dynamic_update_index_in_dim)/dynamic_update_slice | solution.py:69
  102.8 1.9 reshape.200
  104.7 2.0 convolution_bitcast_fusion.9
  113.2 3.6 %dynamic_update_slice.7 = f32[8,32,1024]{2,0,1:T(8,128)} dynamic-update-slice(f32[8,32,1024]{2,0,1:T(8,128)} %get-tuple-element.185, f32[1,32,1024]{2,0,1:T(1,128)S(1)} %broadcast_in_dim.61, s32[]{:T(128)S(6)} %copy.36, s32[]{:T(128)} %constant.91.clone.1..sunk, s32[]{:T(128)} %constant.91.clone.1..sunk) | dynamic-update-slice | bytes 262148 | tf_op jit(solution)/shard_map/while/body/jit(dynamic_update_index_in_dim)/dynamic_update_slice | solution.py:69
  120.6 1.9 reshape.200
  122.5 2.0 convolution_bitcast_fusion.9
  130.9 3.6 %dynamic_update_slice.7 = f32[8,32,1024]{2,0,1:T(8,128)} dynamic-update-slice(f32[8,32,1024]{2,0,1:T(8,128)} %get-tuple-element.185, f32[1,32,1024]{2,0,1:T(1,128)S(1)} %broadcast_in_dim.61, s32[]{:T(128)S(6)} %copy.36, s32[]{:T(128)} %constant.91.clone.1..sunk, s32[]{:T(128)} %constant.91.clone.1..sunk) | dynamic-update-slice | bytes 262148 | tf_op jit(solution)/shard_map/while/body/jit(dynamic_update_index_in_dim)/dynamic_update_slice | solution.py:69
  138.3 1.9 reshape.200
  140.2 2.0 convolution_bitcast_fusion.9
  148.7 3.6 %dynamic_update_slice.7 = f32[8,32,1024]{2,0,1:T(8,128)} dynamic-update-slice(f32[8,32,1024]{2,0,1:T(8,128)} %get-tuple-element.185, f32[1,32,1024]{2,0,1:T(1,128)S(1)} %broadcast_in_dim.61, s32[]{:T(128)S(6)} %copy.36, s32[]{:T(128)} %constant.91.clone.1..sunk, s32[]{:T(128)} %constant.91.clone.1..sunk) | dynamic-update-slice | bytes 262148 | tf_op jit(solution)/shard_map/while/body/jit(dynamic_update_index_in_dim)/dynamic_update_slice | solution.py:69
  154.1 17.4 %all_gather.9 = f32[32,4,1024]{2,0,1:T(8,128)S(1)} all-gather(f32[8,4,1024]{2,0,1:T(8,128)S(1)} %copy.11), channel_id=1, replica_groups=mesh['tgt'=4,'ptr'=8] {'tgt'}, dimensions={0}, use_global_device_ids=true | all-gather | bytes 655360 | tf_op jit(solution)/shard_map/all_gather | solution.py:72
  171.4 19.7 %reduce-scatter.2.cloned.1.call-done = f32[8,4,1024]{2,0,1:T(8,128)} async-done(((f32[8,32,1024]{2,0,1:T(8,128)}), f32[8,4,1024]{2,0,1:T(8,128)}) %reduce-scatter.2.cloned.1.call-update) | async-done | bytes 131088 | tf_op jit(solution)/shard_map/reduce_scatter | solution.py:70
  192.6 12.3 %psum.7 = f32[32,8]{0,1:T(8,128)S(1)} all-reduce(f32[32,8]{0,1:T(8,128)S(1)} %fusion.33), channel_id=1, replica_groups=mesh['tgt'=4,'ptr'=8] {'ptr'}, use_global_device_ids=true, to_apply=%region_4.5 | all-reduce | flops 256 | bytes 2048 | tf_op jit(solution)/shard_map/psum | solution.py:78
  204.9 13.2 %all_gather.10 = f32[32,32]{0,1:T(8,128)S(1)} all-gather(f32[32,8]{0,1:T(8,128)S(1)} %psum.7), channel_id=1, replica_groups=mesh['tgt'=4,'ptr'=8] {'tgt'}, dimensions={1}, use_global_device_ids=true | all-gather | bytes 5120 | tf_op jit(solution)/shard_map/all_gather | solution.py:79
  218.2 2.9 %cholesky.17 = f32[32,32]{1,0:T(8,128)S(1)} custom-call(f32[32,32]{1,0:T(8,128)S(1)} %fusion.43), custom_call_target="Cholesky" | custom-call | tf_op jit(solution)/shard_map/jit(cholesky)/cholesky | solution.py:80
  222.5 2.4 custom-call.7
  225.1 16.1 %all_gather.11 = f32[32,4,1024]{2,0,1:T(8,128)S(1)} all-gather(f32[8,4,1024]{2,0,1:T(8,128)} %reduce-scatter.2.cloned.1.call-done), channel_id=1, replica_groups=mesh['tgt'=4,'ptr'=8] {'tgt'}, dimensions={0}, use_global_device_ids=true | all-gather | bytes 655360 | tf_op jit(solution)/shard_map/all_gather | solution.py:84
  (173 shorter events, 89.2 us)
Async XLA Ops:
  6.5 184.6 %reduce-scatter.2.cloned.1.call-start = ((), (), s32[]{:S(2)}) async-start(), calls=%async_computation.1 | async-start | bytes 1179648 | tf_op jit(solution)/shard_map/reduce_scatter | solution.py:70
  19.0 2.3 copy-start
  36.8 2.3 copy-start
  54.5 2.3 copy-start
  72.3 2.3 copy-start
  90.0 2.3 copy-start
  107.8 2.3 copy-start
  125.5 2.3 copy-start
  143.3 2.3 copy-start
Sparse Core Ops, SparseCore 0:
  152.4 38.6 reduce-scatter.1
where the time goes:
time: 251 us; the launch traced here: 249 us
  local copies, waits for them, and re-layouts  88.3 us (35%)
  blocking collectives  59 us (24%)
  matrix products  45 us (18%)
  other arithmetic  21.3 us (8%)
  waiting for transfers between devices  19.7 us (8%)
  between operations  14.7 us (6%)
    dynamic_update_slice x8, local copies, waits for them, and re-layouts, shards(): every_action = lax.map(action, targets)  28.9 us
    dot_general x16, matrix products, transform(): jnp.dot(matrix, field.reshape(length, -1), precision=HIGHEST_PRECISION)  23.3 us
    reduce_scatter x1, waiting for transfers between devices, shards(): lax.psum_scatter(every_action, 'ptr', scatter_dimension=1, tiled=True)  19.7 us
    all_gather x1, blocking collectives, shards(): target_slab = lax.all_gather(own_slab, 'tgt', axis=0, tiled=True)  17.4 us
    all_gather x1, blocking collectives, shards(): all_actions = lax.all_gather(action_slab, 'tgt', axis=0, tiled=True)  16.1 us
    reshape x8, local copies, waits for them, and re-layouts, action(): spread = jnp.broadcast_to(target_one.reshape(length, length, 1, length),...  15.3 us
    all_gather x1, blocking collectives, shards(): intersection = lax.all_gather(summed_columns, 'tgt', axis=1, tiled=True)  13.2 us
    psum x1, blocking collectives, shards(): summed_columns = lax.psum(columns, 'ptr')  12.3 us
  transfers between devices with their start and end apart: 1, of which 1 were waited for; matrix products, arithmetic and copies ran while one was open for 0% of the time, Pallas kernels for 0%

commit v1 on v0

v1 whole, which is shorter than its diff:
```python
import functools
import math

import jax
import jax.numpy as jnp
import numpy as np
from jax import lax
from jax.experimental import pallas as pl
from jax.experimental.pallas import tpu as pltpu
from jax.sharding import PartitionSpec as P

HIGHEST = lax.Precision.HIGHEST
MESH = pl.DeviceIdType.MESH


def real_dft(values):
    n = len(values)
    if n == 1:
        return [values[0]], [None]
    even_re, even_im = real_dft(values[0::2])
    odd_re, odd_im = real_dft(values[1::2])
    half = n // 2
    re, im = [None] * (half + 1), [None] * (half + 1)
    re[0], re[half] = even_re[0] + odd_re[0], even_re[0] - odd_re[0]
    for k in range(1, half // 2 + 1):
        if 2 * k == half:
            re[k], im[k] = even_re[k], -odd_re[k]
            continue
        c, s = math.cos(2 * math.pi * k / n), -math.sin(2 * math.pi * k / n)
        if 8 * k == n:
            a = c * (odd_re[k] + odd_im[k]) if odd_im[k] is not None else c * odd_re[k]
            b = c * (odd_im[k] - odd_re[k]) if odd_im[k] is not None else -c * odd_re[k]
        else:
            a = c * odd_re[k] - s * odd_im[k]
            b = s * odd_re[k] + c * odd_im[k]
        re[k], re[half - k] = even_re[k] + a, even_re[k] - a
        im[k], im[half - k] = even_im[k] + b, b - even_im[k]
    return re, im


def real_dft_transposed(re, im):
    half = len(re) - 1
    if half == 0:
        return [re[0]]
    n = 2 * half
    quarter = half // 2
    even_re, even_im = [None] * (quarter + 1), [None] * (quarter + 1)
    odd_re, odd_im = [None] * (quarter + 1), [None] * (quarter + 1)
    even_re[0], odd_re[0] = re[0] + re[half], re[0] - re[half]
    for k in range(1, quarter + 1):
        if 2 * k == half:
            even_re[k], odd_re[k] = re[k], -im[k]
            continue
        c, s = math.cos(2 * math.pi * k / n), -math.sin(2 * math.pi * k / n)
        even_re[k], even_im[k] = re[k] + re[half - k], im[k] - im[half - k]
        a, b = re[k] - re[half - k], im[k] + im[half - k]
        if 8 * k == n:
            odd_re[k], odd_im[k] = c * (a - b), c * (a + b)
        else:
            odd_re[k], odd_im[k] = c * a + s * b, c * b - s * a
    values = [None] * n
    values[0::2] = real_dft_transposed(even_re[: quarter + 1], even_im[: quarter + 1])
    values[1::2] = real_dft_transposed(odd_re[: quarter + 1], odd_im[: quarter + 1])
    return values


def flat_dft(values):
    re, im = real_dft(values)
    return re + im[1:-1]


def flat_dft_transposed(modes):
    half = len(modes) // 2
    return real_dft_transposed(modes[: half + 1], [None] + modes[half + 1 :] + [None])


def split_product(field, weights):
    width = field.shape[1]
    high = field.astype(jnp.bfloat16)
    low = (field - high.astype(jnp.float32)).astype(jnp.bfloat16)
    both = jnp.dot(
        jnp.concatenate([high, low], axis=1), weights, preferred_element_type=jnp.float32
    )
    return both[:, :width] + both[:, width:]


def action_kernel(t_ref, psi_ref, occ_ref, weights_ref, table_ref, out_ref, spec):
    length, rows, cells = t_ref.shape
    lanes = psi_ref.shape[2]
    groups = lanes // length
    group_of = lax.broadcasted_iota(jnp.int32, (rows, lanes), 1) // length
    at_group = [group_of == g for g in range(groups)]

    def pick(options):
        chosen = options[0]
        for g in range(1, groups):
            chosen = jnp.where(at_group[g], options[g], chosen)
        return chosen

    def rolled(value, steps):
        steps = steps % groups
        return value if steps == 0 else pltpu.roll(value, steps * length, 1)

    @pl.loop(0, length)
    def forward(x):
        density = []
        for q in range(length // groups):
            v = t_ref[x, :, q * lanes : (q + 1) * lanes]
            turned = [rolled(v, s) for s in range(groups)]
            for g in range(groups):
                y = q * groups + g
                spread = pick([turned[(h - g) % groups] for h in range(groups)])
                density.append(spread * psi_ref[x, y : y + 1, :])
        waves = split_product(jnp.concatenate(density, axis=0), weights_ref[...])
        modes = flat_dft([waves[y * rows : (y + 1) * rows] for y in range(length)])
        for m in range(length):
            spec[x, m] = modes[m]

    @pl.loop(0, length)
    def middle(m):
        modes = flat_dft([spec[x, m] for x in range(length)])
        half = length // 2
        scaled = []
        for i in range(length):
            k = i if i <= half else i - half
            scaled.append(modes[i] * table_ref[m, k : k + 1, :])
        values = flat_dft_transposed(scaled)
        for x in range(length):
            spec[x, m] = values[x]

    @pl.loop(0, length)
    def backward(x):
        values = flat_dft_transposed([spec[x, m] for m in range(length)])
        potential = split_product(jnp.concatenate(values, axis=0), weights_ref[...])
        occ = occ_ref[0:1, :]
        for q in range(length // groups):
            terms = []
            for g in range(groups):
                y = q * groups + g
                terms.append(
                    potential[y * rows : (y + 1) * rows] * (psi_ref[x, y : y + 1, :] * occ)
                )
            total = None
            for s in range(groups):
                part = rolled(pick([terms[(h - s) % groups] for h in range(groups)]), -s)
                total = part if total is None else total + part
            out_ref[x, :, q * lanes : (q + 1) * lanes] = total


def join_kernel(
    tn, pn, part_ref, t_ref, out_ref, rs_buf, t_buf, a_buf, g_buf, inv_ref,
    rs_send, rs_recv, t_send, t_recv, a_send, a_recv, g_send, g_recv,
):
    t, p = lax.axis_index("tgt"), lax.axis_index("ptr")
    slab = part_ref.shape[0] // pn
    rows = part_ref.shape[1]
    cells = part_ref.shape[2]
    all_cells = part_ref.shape[0] * cells
    total_rows = tn * rows
    width = inv_ref.shape[1]

    barrier = pltpu.get_barrier_semaphore()

    @pl.loop(1, tn * pn)
    def greet(d):
        other = lax.rem(t * pn + p + d, tn * pn)
        pl.semaphore_signal(
            barrier, inc=1, device_id=(other // pn, lax.rem(other, pn)), device_id_type=MESH
        )

    pl.semaphore_wait(barrier, tn * pn - 1)

    def rs_copy(q, slot):
        return pltpu.make_async_remote_copy(
            src_ref=part_ref.at[pl.ds(q * slab, slab)], dst_ref=rs_buf.at[slot],
            send_sem=rs_send.at[q], recv_sem=rs_recv.at[slot],
            device_id=(t, q), device_id_type=MESH,
        )

    def t_copy(s, slot):
        return pltpu.make_async_remote_copy(
            src_ref=t_ref.at[pl.ds(p * slab, slab)], dst_ref=t_buf.at[slot],
            send_sem=t_send.at[s], recv_sem=t_recv.at[slot],
            device_id=(s, p), device_id_type=MESH,
        )

    def a_copy(s, slot):
        return pltpu.make_async_remote_copy(
            src_ref=a_buf.at[t], dst_ref=a_buf.at[slot],
            send_sem=a_send.at[s], recv_sem=a_recv.at[slot],
            device_id=(s, p), device_id_type=MESH,
        )

    def g_copy(other, slot):
        return pltpu.make_async_remote_copy(
            src_ref=g_buf.at[t * pn + p], dst_ref=g_buf.at[slot],
            send_sem=g_send.at[other], recv_sem=g_recv.at[slot],
            device_id=(other // pn, lax.rem(other, pn)), device_id_type=MESH,
        )

    for d in range(1, pn):
        rs_copy(lax.rem(p + d, pn), p).start()
    for d in range(1, tn):
        t_copy(lax.rem(t + d, tn), t).start()
    t_buf[t] = t_ref[pl.ds(p * slab, slab)]
    own = part_ref[pl.ds(p * slab, slab)]
    for d in range(1, pn):
        q = lax.rem(p + d, pn)
        rs_copy(q, q).wait_recv()
        own = own + rs_buf[q]
    a_buf[t] = own
    for d in range(1, tn):
        a_copy(lax.rem(t + d, tn), t).start()
    for d in range(1, tn):
        s = lax.rem(t + d, tn)
        t_copy(s, s).wait_recv()
    gram = jnp.zeros((rows, total_rows), jnp.float32)
    for x in range(slab):
        every = jnp.concatenate([t_buf[s, x] for s in range(tn)], axis=0)
        gram = gram + lax.dot_general(
            own[x], every, (((1,), (1,)), ((), ())),
            precision=HIGHEST, preferred_element_type=jnp.float32,
        )
    gram = gram * (1.0 / all_cells)
    g_buf[t * pn + p] = jnp.concatenate(
        [gram, jnp.zeros((rows, width - total_rows), jnp.float32)], axis=1
    )

    @pl.loop(1, tn * pn)
    def spread(d):
        g_copy(lax.rem(t * pn + p + d, tn * pn), t * pn + p).start()

    @pl.loop(1, tn * pn)
    def collect(d):
        other = lax.rem(t * pn + p + d, tn * pn)
        g_copy(other, other).wait_recv()

    blocks = []
    for s in range(tn):
        block = g_buf[s * pn]
        for q in range(1, pn):
            block = block + g_buf[s * pn + q]
        blocks.append(block)
    square = jnp.concatenate(blocks, axis=0)
    padded = jnp.concatenate([square, jnp.zeros((width - total_rows, width), jnp.float32)], axis=0)
    symmetric = 0.5 * (square + jnp.transpose(padded)[:total_rows])
    row_of = lax.broadcasted_iota(jnp.int32, (total_rows, width), 0)
    lane_of = lax.broadcasted_iota(jnp.int32, (total_rows, width), 1)
    work = jnp.where(lane_of == row_of + total_rows, 1.0, symmetric)
    for k in range(total_rows - 1):
        row = work[k : k + 1, :]
        scaled = row / work[k : k + 1, k : k + 1]
        column = jnp.where(row_of > k, work[:, k : k + 1], 0.0)
        work = work - column * scaled
    pivots = jnp.sum(jnp.where(lane_of == row_of, work, 0.0), axis=1, keepdims=True)
    inv_ref[...] = work * (1.0 / jnp.sqrt(pivots))
    mine = inv_ref[pl.ds(pl.multiple_of(t * rows, rows), rows), :][:, total_rows : 2 * total_rows]
    for d in range(1, tn):
        s = lax.rem(t + d, tn)
        a_copy(s, s).wait_recv()
    for x in range(slab):
        every = jnp.concatenate([a_buf[s, x] for s in range(tn)], axis=0)
        out_ref[x] = jnp.dot(mine, every, precision=HIGHEST, preferred_element_type=jnp.float32)

    for d in range(1, pn):
        rs_copy(lax.rem(p + d, pn), p).wait_send()
    for d in range(1, tn):
        t_copy(lax.rem(t + d, tn), t).wait_send()
        a_copy(lax.rem(t + d, tn), t).wait_send()

    @pl.loop(1, tn * pn)
    def drain(d):
        g_copy(lax.rem(t * pn + p + d, tn * pn), t * pn + p).wait_send()


def constants(length, groups):
    i = np.arange(length)
    phase = 2.0 * np.pi / length * (i[:, None] * i[None, :] % length)
    cas = np.kron(np.eye(groups), np.cos(phase) + np.sin(phase)).astype(np.float32)
    high = cas.astype(jnp.bfloat16)
    low = (cas - high.astype(np.float32)).astype(jnp.bfloat16)
    weights = np.concatenate([np.concatenate([high, low], 1)] * 2, 0)
    signed = np.where(i < length // 2, i, i - length)
    half = length // 2
    k = np.arange(half + 1)
    wave = (2.0 * np.pi / length) ** 2
    total = wave * ((k**2)[:, None, None] + (k**2)[None, :, None] + (signed**2)[None, None, :])
    coulomb = np.where(total > 0, 4 * np.pi / np.where(total > 0, total, 1.0), 0.0)
    fold = np.where((k == 0) | (k == half), 1.0, 2.0)
    coulomb = coulomb * fold[:, None, None] * fold[None, :, None] / length**3
    order = np.concatenate([np.arange(half + 1), np.arange(1, half)])
    table = np.tile(coulomb[order], (1, 1, groups)).astype(np.float32)
    return weights, table


def shards(tn, pn, targets, partners, occupied, retained):
    rows, length, cells = targets.shape
    lanes = partners.shape[2]
    groups = lanes // length
    slab = length // pn
    weights, table = constants(length, groups)
    per_block = groups // occupied.shape[0]
    occupancy = 0.25 + 0.75 * jnp.repeat(occupied.astype(jnp.float32), per_block * length)
    planes = jnp.transpose(targets, (1, 0, 2))
    vmem = pl.BlockSpec(memory_space=pltpu.VMEM)
    partial = pl.pallas_call(
        action_kernel,
        out_shape=jax.ShapeDtypeStruct((length, rows, cells), jnp.float32),
        in_specs=[vmem] * 5,
        out_specs=vmem,
        scratch_shapes=[pltpu.VMEM((length, length, rows, lanes), jnp.float32)],
        name="actions",
    )(planes, partners, occupancy[None, :], jnp.asarray(weights), jnp.asarray(table))
    total_rows = tn * rows
    width = -(-2 * total_rows // 128) * 128
    dma = pltpu.SemaphoreType.DMA
    block = pltpu.VMEM((tn, slab, rows, cells), jnp.float32)
    result = pl.pallas_call(
        functools.partial(join_kernel, tn, pn),
        out_shape=jax.ShapeDtypeStruct((slab, rows, cells), jnp.float32),
        in_specs=[vmem] * 2,
        out_specs=vmem,
        scratch_shapes=[
            pltpu.VMEM((pn, slab, rows, cells), jnp.float32),
            block,
            block,
            pltpu.VMEM((tn * pn, rows, width), jnp.float32),
            pltpu.VMEM((total_rows, width), jnp.float32),
            dma((pn,)), dma((pn,)), dma((tn,)), dma((tn,)),
            dma((tn,)), dma((tn,)), dma((tn * pn,)), dma((tn * pn,)),
        ],
        compiler_params=pltpu.CompilerParams(collective_id=0, has_side_effects=True),
        name="join",
    )(partial, planes)
    global_rows = lax.axis_index("tgt") * rows + jnp.arange(rows, dtype=jnp.int32)
    keeping = (global_rows < retained[0]).astype(jnp.float32)
    return jnp.transpose(result, (1, 0, 2)) * keeping[:, None, None]


def solution(mesh):
    return jax.shard_map(
        functools.partial(shards, mesh.shape["tgt"], mesh.shape["ptr"]),
        mesh=mesh,
        in_specs=(P("tgt", None, None), P(None, None, "ptr"), P("ptr"), P()),
        out_specs=P("tgt", "ptr", None),
        check_vma=False,
    )
```

time: 251 us -> 70.5 us (0.28)
  local copies, waits for them, and re-layouts: 88.3 us -> 4.09 us
  Pallas kernels: 0 us -> 63.9 us
  blocking collectives: 59 us -> 0 us
  matrix products: 45 us -> 0 us
  other arithmetic: 21.3 us -> 0.99 us
  waiting for transfers between devices: 19.7 us -> 0 us
  between operations: 14.7 us -> 1.33 us
    pallas_call x0 -> x2, Pallas kernels: none -> 63.9 us  [the longest x1 41.3 us: shards(): pl.pallas_call(functools.partial(join_kernel, tn, pn), out_shape=jax.Shap...]
    all_gather x3 -> x0, blocking collectives: 46.7 us -> none  [the longest x1 17.4 us: shards(): target_slab = lax.all_gather(own_slab, 'tgt', axis=0, tiled=True)]
    dot_general x50 -> x0, matrix products: 44.8 us -> none  [the longest x16 23.3 us: transform(): jnp.dot(matrix, field.reshape(length, -1), precision=HIGHEST_PRECISION)]
    reshape x24 -> x0, local copies, waits for them, and re-layouts: 29.6 us -> none  [the longest x8 15.3 us: action(): spread = jnp.broadcast_to(target_one.reshape(length, length, 1, length),...]
    dynamic_update_slice x8 -> x0, local copies, waits for them, and re-layouts: 28.9 us -> none  [shards(): every_action = lax.map(action, targets)]
    reduce_scatter x1 -> x0, waiting for transfers between devices: 19.7 us -> none  [shards(): lax.psum_scatter(every_action, 'ptr', scatter_dimension=1, tiled=True)]
    broadcast_in_dim x32 -> x1, local copies, waits for them, and re-layouts: 17.6 us -> 0.52 us  [shards(): occupancy[None, :]]
    psum x1 -> x0, blocking collectives: 12.3 us -> none  [shards(): summed_columns = lax.psum(columns, 'ptr')]
  transfers between devices with their start and end apart: 1 -> 0, of which waited for: 1 -> 0; matrix products, arithmetic and copies ran while one was open for 0% -> 0% of each run, Pallas kernels for 0% -> 0%
where the time goes in v1:
time: 70.5 us; the launch traced here: 70.3 us
  Pallas kernels  63.9 us (91%)
  local copies, waits for them, and re-layouts  4.09 us (6%)
  between operations  1.33 us (2%)
  other arithmetic  0.99 us (1%)
    pallas_call x1, Pallas kernels, shards(): pl.pallas_call(functools.partial(join_kernel, tn, pn), out_shape=jax.Shap...  41.3 us
    pallas_call x1, Pallas kernels, shards(): pl.pallas_call(action_kernel, out_shape=jax.ShapeDtypeStruct((length, row...  22.5 us
    unnamed x1, local copies, waits for them, and re-layouts  2.82 us

profile of v1, /device:TPU:0, one launch (start us, length us, event | category | flops | bytes accessed | tf_op | source)
XLA Modules:
  0.0 70.3 jit_solution(17123464019664490949)
XLA Ops:
  0.0 2.8 %copy.10 = f32[8,32,1024]{2,0,1:T(8,128)} copy(f32[8,32,1024]{2,1,0:T(8,128)} %param.6) | data formatting | bytes 2097152 | tf_op args[0]
  3.5 0.5 broadcast_in_dim.2.occ_ref
  4.0 22.5 %actions.1.part_ref = f32[32,8,1024]{2,1,0:T(8,128)} custom-call(f32[32,8,1024]{2,1,0:T(8,128)} %bitcast.8, f32[32,32,128]{2,1,0:T(8,128)} %psi_ref.1, f32[1,128]{1,0:T(1,128)} %broadcast_in_dim.2.occ_ref, bf16[256,256]{1,0:T(8,128)(2,1)} %constant.17.clone.weights_ref, f32[32,17,128]{2,1,0:T(8,128)} %constant.18.clone.table_ref), custom_call_target="tpu_custom_call" | custom-call | tf_op jit(solution)/shard_map/actions/pallas_call | solution.py:306
  26.5 41.3 %join.1 = f32[4,8,1024]{2,1,0:T(8,128)} custom-call(f32[32,8,1024]{2,1,0:T(8,128)} %actions.1.part_ref, f32[32,8,1024]{2,1,0:T(8,128)} %bitcast.9), custom_call_target="tpu_custom_call" | custom-call | tf_op jit(solution)/shard_map/join/pallas_call | solution.py:318
  68.5 1.0 %multiply_bitcast_fusion = f32[8,4,1024]{2,0,1:T(8,128)S(1)} fusion(f32[4,8,1024]{2,1,0:T(8,128)} %join.1, f32[8]{0:T(128)S(1)} %compare_convert_fusion), kind=kLoop, calls=%fused_computation.1 | loop fusion | flops 32768 | bytes 262176 | tf_op jit(solution)/shard_map/mul | solution.py:337
  69.5 0.7 %copy.8 = f32[8,4,1024]{2,1,0:T(4,128)} copy(f32[8,4,1024]{2,0,1:T(8,128)S(1)} %multiply_bitcast_fusion) | data formatting | bytes 262144 | tf_op jit(solution)/shard_map/mul | solution.py:337
  (1 shorter events, 0.0 us)

commit v2 on v1

v2 whole, which is shorter than its diff:
```python
import functools
import math

import jax
import jax.numpy as jnp
import numpy as np
from jax import lax
from jax.experimental import pallas as pl
from jax.experimental.pallas import tpu as pltpu
from jax.sharding import PartitionSpec as P

HIGHEST = lax.Precision.HIGHEST
MESH = pl.DeviceIdType.MESH
FORWARD = 4
BACKWARD = 4


def real_dft(values):
    n = len(values)
    if n == 1:
        return [values[0]], [None]
    even_re, even_im = real_dft(values[0::2])
    odd_re, odd_im = real_dft(values[1::2])
    half = n // 2
    re, im = [None] * (half + 1), [None] * (half + 1)
    re[0], re[half] = even_re[0] + odd_re[0], even_re[0] - odd_re[0]
    for k in range(1, half // 2 + 1):
        if 2 * k == half:
            re[k], im[k] = even_re[k], -odd_re[k]
            continue
        c, s = math.cos(2 * math.pi * k / n), -math.sin(2 * math.pi * k / n)
        if 8 * k == n:
            a = c * (odd_re[k] + odd_im[k]) if odd_im[k] is not None else c * odd_re[k]
            b = c * (odd_im[k] - odd_re[k]) if odd_im[k] is not None else -c * odd_re[k]
        else:
            a = c * odd_re[k] - s * odd_im[k]
            b = s * odd_re[k] + c * odd_im[k]
        re[k], re[half - k] = even_re[k] + a, even_re[k] - a
        im[k], im[half - k] = even_im[k] + b, b - even_im[k]
    return re, im


def real_dft_transposed(re, im):
    half = len(re) - 1
    if half == 0:
        return [re[0]]
    n = 2 * half
    quarter = half // 2
    even_re, even_im = [None] * (quarter + 1), [None] * (quarter + 1)
    odd_re, odd_im = [None] * (quarter + 1), [None] * (quarter + 1)
    even_re[0], odd_re[0] = re[0] + re[half], re[0] - re[half]
    for k in range(1, quarter + 1):
        if 2 * k == half:
            even_re[k], odd_re[k] = re[k], -im[k]
            continue
        c, s = math.cos(2 * math.pi * k / n), -math.sin(2 * math.pi * k / n)
        even_re[k], even_im[k] = re[k] + re[half - k], im[k] - im[half - k]
        a, b = re[k] - re[half - k], im[k] + im[half - k]
        if 8 * k == n:
            odd_re[k], odd_im[k] = c * (a - b), c * (a + b)
        else:
            odd_re[k], odd_im[k] = c * a + s * b, c * b - s * a
    values = [None] * n
    values[0::2] = real_dft_transposed(even_re[: quarter + 1], even_im[: quarter + 1])
    values[1::2] = real_dft_transposed(odd_re[: quarter + 1], odd_im[: quarter + 1])
    return values


def flat_dft(values):
    re, im = real_dft(values)
    return re + im[1:-1]


def flat_dft_transposed(modes):
    half = len(modes) // 2
    return real_dft_transposed(modes[: half + 1], [None] + modes[half + 1 :] + [None])


def split_product(field, weights):
    width = field.shape[1]
    high = field.astype(jnp.bfloat16)
    low = (field - high.astype(jnp.float32)).astype(jnp.bfloat16)
    both = jnp.dot(
        jnp.concatenate([high, low], axis=1), weights, preferred_element_type=jnp.float32
    )
    return both[:, :width] + both[:, width:]


def kernel(
    tn, pn, t_hbm, psi_ref, weights_ref, table_ref, occupied_ref, retained_ref, out_ref,
    planes, spec, part, rs_buf, t_buf, a_buf, gram_ref, g_buf, inv_ref,
    load_sem, rs_send, rs_recv, t_send, t_recv, a_send, a_recv, g_send, g_recv,
):
    t, p = lax.axis_index("tgt"), lax.axis_index("ptr")
    length, rows, cells = planes.shape
    lanes = psi_ref.shape[2]
    groups = lanes // length
    slab = length // pn
    all_cells = length * cells
    total_rows = tn * rows
    width = inv_ref.shape[1]
    me = t * pn + p
    devices = tn * pn

    loads = [
        pltpu.make_async_copy(t_hbm.at[a], planes.at[:, a, :], load_sem.at[a]) for a in range(rows)
    ]
    for load in loads:
        load.start()

    barrier = pltpu.get_barrier_semaphore()

    @pl.loop(1, devices)
    def greet(d):
        other = lax.rem(me + d, devices)
        pl.semaphore_signal(
            barrier, inc=1, device_id=(other // pn, lax.rem(other, pn)), device_id_type=MESH
        )

    pl.semaphore_wait(barrier, devices - 1)
    for load in loads:
        load.wait()

    def rs_copy(q, slot, r):
        return pltpu.make_async_remote_copy(
            src_ref=part.at[q * slab + r], dst_ref=rs_buf.at[slot, r],
            send_sem=rs_send.at[q, r], recv_sem=rs_recv.at[slot, r],
            device_id=(t, q), device_id_type=MESH,
        )

    def t_copy(s, slot):
        return pltpu.make_async_remote_copy(
            src_ref=planes.at[pl.ds(p * slab, slab)], dst_ref=t_buf.at[slot],
            send_sem=t_send.at[s], recv_sem=t_recv.at[slot],
            device_id=(s, p), device_id_type=MESH,
        )

    def a_copy(s, slot, r):
        return pltpu.make_async_remote_copy(
            src_ref=a_buf.at[t, r], dst_ref=a_buf.at[slot, r],
            send_sem=a_send.at[s, r], recv_sem=a_recv.at[slot, r],
            device_id=(s, p), device_id_type=MESH,
        )

    def g_copy(other, slot):
        return pltpu.make_async_remote_copy(
            src_ref=g_buf.at[me], dst_ref=g_buf.at[slot],
            send_sem=g_send.at[other], recv_sem=g_recv.at[slot],
            device_id=(other // pn, lax.rem(other, pn)), device_id_type=MESH,
        )

    for d in range(1, tn):
        t_copy(lax.rem(t + d, tn), t).start()

    group_of = lax.broadcasted_iota(jnp.int32, (rows, lanes), 1) // length
    at_group = [group_of == g for g in range(groups)]
    per_block = groups // occupied_ref.shape[0]
    occ = 0.25 + 0.75 * occupied_ref[0].astype(jnp.float32) * jnp.ones((rows, lanes), jnp.float32)
    for i in range(1, occupied_ref.shape[0]):
        level = 0.25 + 0.75 * occupied_ref[i].astype(jnp.float32)
        occ = jnp.where(group_of >= i * per_block, level, occ)

    def pick(options):
        chosen = options[0]
        for g in range(1, groups):
            chosen = jnp.where(at_group[g], options[g], chosen)
        return chosen

    def rolled(value, steps):
        steps = steps % groups
        return value if steps == 0 else pltpu.roll(value, steps * length, 1)

    plane_rows = length * rows

    @pl.loop(0, length // FORWARD)
    def forward(i):
        density = []
        for j in range(FORWARD):
            x = i * FORWARD + j
            for q in range(length // groups):
                v = planes[x, :, q * lanes : (q + 1) * lanes]
                turned = [rolled(v, s) for s in range(groups)]
                for g in range(groups):
                    y = q * groups + g
                    spread = pick([turned[(h - g) % groups] for h in range(groups)])
                    density.append(spread * psi_ref[x, y : y + 1, :])
        waves = split_product(jnp.concatenate(density, axis=0), weights_ref[...])
        for j in range(FORWARD):
            wave = waves[j * plane_rows : (j + 1) * plane_rows]
            modes = flat_dft([wave[y * rows : (y + 1) * rows] for y in range(length)])
            for m in range(length):
                spec[i * FORWARD + j, m] = modes[m]

    @pl.loop(0, length)
    def middle(m):
        modes = flat_dft([spec[x, m] for x in range(length)])
        half = length // 2
        scaled = []
        for i in range(length):
            k = i if i <= half else i - half
            scaled.append(modes[i] * table_ref[m, k : k + 1, :])
        values = flat_dft_transposed(scaled)
        for x in range(length):
            spec[x, m] = values[x]

    gram_ref[...] = jnp.zeros_like(gram_ref)

    def reduce_round(r):
        own = part[p * slab + r]
        for d in range(1, pn):
            q = lax.rem(p + d, pn)
            rs_copy(q, q, r).wait_recv()
            own = own + rs_buf[q, r]
        a_buf[t, r] = own
        for d in range(1, tn):
            a_copy(lax.rem(t + d, tn), t, r).start()
        every = jnp.concatenate([t_buf[s, r] for s in range(tn)], axis=0)
        gram_ref[...] += lax.dot_general(
            own, every, (((1,), (1,)), ((), ())),
            precision=HIGHEST, preferred_element_type=jnp.float32,
        )

    @pl.loop(0, slab)
    def rounds(r):
        @pl.loop(0, pn // BACKWARD)
        def backward(i):
            owners = [lax.rem(p + 1 + i * BACKWARD + j, pn) for j in range(BACKWARD)]
            values = []
            for q in owners:
                values += flat_dft_transposed([spec[q * slab + r, m] for m in range(length)])
            potentials = split_product(jnp.concatenate(values, axis=0), weights_ref[...])
            for j, owner in enumerate(owners):
                x = owner * slab + r
                potential = potentials[j * plane_rows : (j + 1) * plane_rows]
                for q in range(length // groups):
                    terms = []
                    for g in range(groups):
                        y = q * groups + g
                        terms.append(potential[y * rows : (y + 1) * rows] * psi_ref[x, y : y + 1, :])
                    total = None
                    for s in range(groups):
                        chosen = pick([terms[(h - s) % groups] for h in range(groups)])
                        moved = rolled(chosen * occ, -s)
                        total = moved if total is None else total + moved
                    part[x, :, q * lanes : (q + 1) * lanes] = total
            for j in range(BACKWARD):
                @pl.when(i * BACKWARD + j < pn - 1)
                def send():
                    rs_copy(owners[j], p, r).start()

        @pl.when(r == 0)
        def targets_in():
            t_buf[t] = planes[pl.ds(p * slab, slab)]
            for d in range(1, tn):
                s = lax.rem(t + d, tn)
                t_copy(s, s).wait_recv()

        @pl.when(r > 0)
        def earlier():
            reduce_round(r - 1)

    reduce_round(slab - 1)

    gram = gram_ref[...] * (1.0 / all_cells)
    g_buf[me] = jnp.concatenate(
        [gram, jnp.zeros((rows, width - total_rows), jnp.float32)], axis=1
    )

    @pl.loop(1, devices)
    def spread_gram(d):
        g_copy(lax.rem(me + d, devices), me).start()

    @pl.loop(1, devices)
    def collect(d):
        other = lax.rem(me + d, devices)
        g_copy(other, other).wait_recv()

    blocks = []
    for s in range(tn):
        block = g_buf[s * pn]
        for q in range(1, pn):
            block = block + g_buf[s * pn + q]
        blocks.append(block)
    square = jnp.concatenate(blocks, axis=0)
    padded = jnp.concatenate([square, jnp.zeros((width - total_rows, width), jnp.float32)], axis=0)
    symmetric = 0.5 * (square + jnp.transpose(padded)[:total_rows])
    row_of = lax.broadcasted_iota(jnp.int32, (total_rows, width), 0)
    lane_of = lax.broadcasted_iota(jnp.int32, (total_rows, width), 1)
    work = jnp.where(lane_of == row_of + total_rows, 1.0, symmetric)
    for k in range(total_rows - 1):
        row = work[k : k + 1, :]
        scaled = row / work[k : k + 1, k : k + 1]
        column = jnp.where(row_of > k, work[:, k : k + 1], 0.0)
        work = work - column * scaled
    pivots = jnp.sum(jnp.where(lane_of == row_of, work, 0.0), axis=1, keepdims=True)
    keeping = (row_of < retained_ref[0]).astype(jnp.float32)
    inv_ref[...] = work * (1.0 / jnp.sqrt(pivots)) * keeping
    mine = inv_ref[pl.ds(pl.multiple_of(t * rows, rows), rows), :][:, total_rows : 2 * total_rows]
    for d in range(1, tn):
        s = lax.rem(t + d, tn)
        for r in range(slab):
            a_copy(s, s, r).wait_recv()
    for x in range(slab):
        every = jnp.concatenate([a_buf[s, x] for s in range(tn)], axis=0)
        out_ref[:, x, :] = jnp.dot(
            mine, every, precision=HIGHEST, preferred_element_type=jnp.float32
        )

    for d in range(1, pn):
        for r in range(slab):
            rs_copy(lax.rem(p + d, pn), p, r).wait_send()
    for d in range(1, tn):
        t_copy(lax.rem(t + d, tn), t).wait_send()
        for r in range(slab):
            a_copy(lax.rem(t + d, tn), t, r).wait_send()

    @pl.loop(1, devices)
    def drain(d):
        g_copy(lax.rem(me + d, devices), me).wait_send()


def constants(length, groups):
    i = np.arange(length)
    phase = 2.0 * np.pi / length * (i[:, None] * i[None, :] % length)
    cas = np.kron(np.eye(groups), np.cos(phase) + np.sin(phase)).astype(np.float32)
    high = cas.astype(jnp.bfloat16)
    low = (cas - high.astype(np.float32)).astype(jnp.bfloat16)
    weights = np.concatenate([np.concatenate([high, low], 1)] * 2, 0)
    signed = np.where(i < length // 2, i, i - length)
    half = length // 2
    k = np.arange(half + 1)
    wave = (2.0 * np.pi / length) ** 2
    total = wave * ((k**2)[:, None, None] + (k**2)[None, :, None] + (signed**2)[None, None, :])
    coulomb = np.where(total > 0, 4 * np.pi / np.where(total > 0, total, 1.0), 0.0)
    fold = np.where((k == 0) | (k == half), 1.0, 2.0)
    coulomb = coulomb * fold[:, None, None] * fold[None, :, None] / length**3
    order = np.concatenate([np.arange(half + 1), np.arange(1, half)])
    table = np.tile(coulomb[order], (1, 1, groups)).astype(np.float32)
    return weights, table


def shards(tn, pn, targets, partners, occupied, retained):
    rows, length, cells = targets.shape
    lanes = partners.shape[2]
    groups = lanes // length
    slab = length // pn
    weights, table = constants(length, groups)
    total_rows = tn * rows
    width = -(-2 * total_rows // 128) * 128
    vmem = pl.BlockSpec(memory_space=pltpu.VMEM)
    smem = pl.BlockSpec(memory_space=pltpu.SMEM)
    dma = pltpu.SemaphoreType.DMA
    planes = pltpu.VMEM((length, rows, cells), jnp.float32)
    block = pltpu.VMEM((tn, slab, rows, cells), jnp.float32)
    return pl.pallas_call(
        functools.partial(kernel, tn, pn),
        out_shape=jax.ShapeDtypeStruct((rows, slab, cells), jnp.float32),
        in_specs=[pl.BlockSpec(memory_space=pl.ANY), vmem, vmem, vmem, smem, smem],
        out_specs=vmem,
        scratch_shapes=[
            planes,
            pltpu.VMEM((length, length, rows, lanes), jnp.float32),
            planes,
            pltpu.VMEM((pn, slab, rows, cells), jnp.float32),
            block,
            block,
            pltpu.VMEM((rows, total_rows), jnp.float32),
            pltpu.VMEM((tn * pn, rows, width), jnp.float32),
            pltpu.VMEM((total_rows, width), jnp.float32),
            dma((rows,)), dma((pn, slab)), dma((pn, slab)), dma((tn,)), dma((tn,)),
            dma((tn, slab)), dma((tn, slab)), dma((tn * pn,)), dma((tn * pn,)),
        ],
        compiler_params=pltpu.CompilerParams(collective_id=0, has_side_effects=True),
        name="exchange",
    )(targets, partners, jnp.asarray(weights), jnp.asarray(table), occupied, retained)


def solution(mesh):
    return jax.shard_map(
        functools.partial(shards, mesh.shape["tgt"], mesh.shape["ptr"]),
        mesh=mesh,
        in_specs=(P("tgt", None, None), P(None, None, "ptr"), P("ptr"), P()),
        out_specs=P("tgt", "ptr", None),
        check_vma=False,
    )
```

time: 70.5 us -> 47.7 us (0.68)
  Pallas kernels: 63.9 us -> 44.7 us
  local copies, waits for them, and re-layouts: 4.09 us -> 1.57 us
  other arithmetic: 0.99 us -> 0 us
    pallas_call x2 -> x1, Pallas kernels: 63.9 us -> 44.7 us  [shards(): pl.pallas_call(functools.partial(kernel, tn, pn), out_shape=jax.ShapeDtyp...]
    unnamed x1, local copies, waits for them, and re-layouts: 2.82 us -> 1.57 us
    mul x1 -> x0, other arithmetic: 0.98 us -> none  [shards(): return jnp.transpose(result, (1, 0, 2)) * keeping[:, None, None]]
    mul x1 -> x0, local copies, waits for them, and re-layouts: 0.74 us -> none  [shards(): return jnp.transpose(result, (1, 0, 2)) * keeping[:, None, None]]
where the time goes in v2:
time: 47.7 us; the launch traced here: 47.5 us
  Pallas kernels  44.7 us (94%)
  local copies, waits for them, and re-layouts  1.57 us (3%)
  between operations  1.3 us (3%)
    pallas_call x1, Pallas kernels, shards(): pl.pallas_call(functools.partial(kernel, tn, pn), out_shape=jax.ShapeDtyp...  44.7 us
    unnamed x1, local copies, waits for them, and re-layouts  1.57 us

profile of v2, /device:TPU:0, one launch (start us, length us, event | category | flops | bytes accessed | tf_op | source)
XLA Modules:
  0.0 47.5 jit_solution(6845879164218523770)
XLA Ops:
  1.3 44.7 %exchange.1 = f32[8,4,1024]{2,1,0:T(4,128)} custom-call(f32[8,32,1024]{2,1,0:T(8,128)} %t_hbm.1, f32[32,32,128]{2,1,0:T(8,128)} %psi_ref.1, bf16[256,256]{1,0:T(8,128)(2,1)} %constant.4.clone.weights_ref, f32[32,17,128]{2,1,0:T(8,128)} %constant.5.clone.table_ref, s32[1]{0:T(128)S(6)} %copy.8.occupied_ref, s32[1]{0:T(128)S(6)} %copy.9.retained_ref), custom_call_target="tpu_custom_call" | custom-call | tf_op jit(solution)/shard_map/exchange/pallas_call | solution.py:355
  46.0 1.6 %copy.10 = f32[8,4,1024]{2,1,0:T(4,128)} copy(f32[8,4,1024]{2,1,0:T(4,128)} %exchange.1) | data formatting | bytes 262144

commit v3 on v2

--- a/solution.py
+++ b/solution.py
@@ -88,8 +88,8 @@
 
 def kernel(
     tn, pn, t_hbm, psi_ref, weights_ref, table_ref, occupied_ref, retained_ref, out_ref,
-    planes, spec, part, rs_buf, t_buf, a_buf, gram_ref, g_buf, inv_ref,
-    load_sem, rs_send, rs_recv, t_send, t_recv, a_send, a_recv, g_send, g_recv,
+    planes, spec, part, pair_buf, rs_buf, t_buf, a_buf, gram_ref, g_buf, inv_ref,
+    load_sem, pair_send, pair_recv, rs_send, rs_recv, t_send, t_recv, a_send, a_recv, g_send, g_recv,
 ):
     t, p = lax.axis_index("tgt"), lax.axis_index("ptr")
     length, rows, cells = planes.shape
@@ -101,6 +101,9 @@
     width = inv_ref.shape[1]
     me = t * pn + p
     devices = tn * pn
+    chips = pn // 2
+    chip, core = p // 2, lax.rem(p, 2)
+    partner = p + 1 - 2 * core
 
     loads = [
         pltpu.make_async_copy(t_hbm.at[a], planes.at[:, a, :], load_sem.at[a]) for a in range(rows)
@@ -121,26 +124,59 @@
     for load in loads:
         load.wait()
 
-    def rs_copy(q, slot, r):
+    def pair_copy(q, r):
+        return pltpu.make_async_remote_copy(
+            src_ref=part.at[q * slab + r], dst_ref=pair_buf.at[q // 2, r],
+            send_sem=pair_send.at[q // 2, r], recv_sem=pair_recv.at[q // 2, r],
+            device_id=(t, partner), device_id_type=MESH,
+        )
+
+    def rs_copy(c, slot, r):
+        q = 2 * c + core
         return pltpu.make_async_remote_copy(
             src_ref=part.at[q * slab + r], dst_ref=rs_buf.at[slot, r],
-            send_sem=rs_send.at[q, r], recv_sem=rs_recv.at[slot, r],
+            send_sem=rs_send.at[c, r], recv_sem=rs_recv.at[slot, r],
             device_id=(t, q), device_id_type=MESH,
         )
 
-    def t_copy(s, slot):
+    def t_copy(s, side):
         return pltpu.make_async_remote_copy(
-            src_ref=planes.at[pl.ds(p * slab, slab)], dst_ref=t_buf.at[slot],
-            send_sem=t_send.at[s], recv_sem=t_recv.at[slot],
-            device_id=(s, p), device_id_type=MESH,
-        )
-
-    def a_copy(s, slot, r):
+            src_ref=t_buf.at[s], dst_ref=t_buf.at[s],
+            send_sem=t_send.at[(side + 1) // 2, s], recv_sem=t_recv.at[s],
+            device_id=(t + side, p), device_id_type=MESH,
+        )
+
+    def a_copy(s, side, r):
         return pltpu.make_async_remote_copy(
-            src_ref=a_buf.at[t, r], dst_ref=a_buf.at[slot, r],
-            send_sem=a_send.at[s, r], recv_sem=a_recv.at[slot, r],
-            device_id=(s, p), device_id_type=MESH,
-        )
+            src_ref=a_buf.at[s, r], dst_ref=a_buf.at[s, r],
+            send_sem=a_send.at[(side + 1) // 2, s, r], recv_sem=a_recv.at[s, r],
+            device_id=(t + side, p), device_id_type=MESH,
+        )
+
+    def relay(copy, hop, *at):
+        for side in (-1, 1):
+            s = t - side * (hop - 1)
+            held = (s >= 0) & (s < tn)
+            if hop > 1:
+
+                @pl.when(held)
+                def arrived():
+                    copy(s, side, *at).wait_recv()
+
+            if hop < tn:
+
+                @pl.when(held & (t + side >= 0) & (t + side < tn))
+                def onward():
+                    copy(s, side, *at).start()
+
+    def relayed(copy, *at):
+        for side in (-1, 1):
+            for hop in range(1, tn):
+                s = t - side * (hop - 1)
+
+                @pl.when((s >= 0) & (s < tn) & (t + side >= 0) & (t + side < tn))
+                def sent():
+                    copy(s, side, *at).wait_send()
 
     def g_copy(other, slot):
         return pltpu.make_async_remote_copy(
@@ -149,8 +185,8 @@
             device_id=(other // pn, lax.rem(other, pn)), device_id_type=MESH,
         )
 
-    for d in range(1, tn):
-        t_copy(lax.rem(t + d, tn), t).start()
+    t_buf[t] = planes[pl.ds(p * slab, slab)]
+    relay(t_copy, 1)
 
     group_of = lax.broadcasted_iota(jnp.int32, (rows, lanes), 1) // length
     at_group = [group_of == g for g in range(groups)]
@@ -191,6 +227,8 @@
             for m in range(length):
                 spec[i * FORWARD + j, m] = modes[m]
 
+    relay(t_copy, 2)
+
     @pl.loop(0, length)
     def middle(m):
         modes = flat_dft([spec[x, m] for x in range(length)])
@@ -204,16 +242,29 @@
             spec[x, m] = values[x]
 
     gram_ref[...] = jnp.zeros_like(gram_ref)
+    relay(t_copy, 3)
+
+    def relay_step(e):
+        for hop in range(2, tn + 1):
+            r = e - hop + 1
+            if isinstance(e, int):
+                if 0 <= r < slab:
+                    relay(a_copy, hop, r)
+            else:
+
+                @pl.when(r >= 0)
+                def earlier_round():
+                    relay(a_copy, hop, r)
 
     def reduce_round(r):
-        own = part[p * slab + r]
-        for d in range(1, pn):
-            q = lax.rem(p + d, pn)
-            rs_copy(q, q, r).wait_recv()
-            own = own + rs_buf[q, r]
+        own = part[p * slab + r] + pair_buf[chip, r]
+        for d in range(1, chips):
+            c = lax.rem(chip + d, chips)
+            rs_copy(c, c, r).wait_recv()
+            own = own + rs_buf[c, r]
         a_buf[t, r] = own
-        for d in range(1, tn):
-            a_copy(lax.rem(t + d, tn), t, r).start()
+        relay(a_copy, 1, r)
+        relay_step(r)
         every = jnp.concatenate([t_buf[s, r] for s in range(tn)], axis=0)
         gram_ref[...] += lax.dot_general(
             own, every, (((1,), (1,)), ((), ())),
@@ -224,7 +275,12 @@
     def rounds(r):
         @pl.loop(0, pn // BACKWARD)
         def backward(i):
-            owners = [lax.rem(p + 1 + i * BACKWARD + j, pn) for j in range(BACKWARD)]
+            away = i < chips // BACKWARD
+            first = lax.rem(i * BACKWARD, chips)
+            side = jnp.where(away, 1 - core, core)
+            owners = [
+                2 * lax.rem(chip + 1 + first + j, chips) + side for j in range(BACKWARD)
+            ]
             values = []
             for q in owners:
                 values += flat_dft_transposed([spec[q * slab + r, m] for m in range(length)])
@@ -243,17 +299,27 @@
                         moved = rolled(chosen * occ, -s)
                         total = moved if total is None else total + moved
                     part[x, :, q * lanes : (q + 1) * lanes] = total
-            for j in range(BACKWARD):
-                @pl.when(i * BACKWARD + j < pn - 1)
-                def send():
-                    rs_copy(owners[j], p, r).start()
+
+            @pl.when(away)
+            def to_partner():
+                for owner in owners:
+                    pair_copy(owner, r).start()
+
+            @pl.when(jnp.logical_not(away))
+            def to_owners():
+                for j, owner in enumerate(owners):
+                    pair_copy(owner, r).wait_recv()
+
+                    @pl.when(first + j < chips - 1)
+                    def send():
+                        x = owner * slab + r
+                        part[x] = part[x] + pair_buf[owner // 2, r]
+                        rs_copy(owner // 2, chip, r).start()
 
         @pl.when(r == 0)
         def targets_in():
-            t_buf[t] = planes[pl.ds(p * slab, slab)]
-            for d in range(1, tn):
-                s = lax.rem(t + d, tn)
-                t_copy(s, s).wait_recv()
+            for hop in range(4, tn + 1):
+                relay(t_copy, hop)
 
         @pl.when(r > 0)
         def earlier():
@@ -262,26 +328,32 @@
     reduce_round(slab - 1)
 
     gram = gram_ref[...] * (1.0 / all_cells)
-    g_buf[me] = jnp.concatenate(
-        [gram, jnp.zeros((rows, width - total_rows), jnp.float32)], axis=1
-    )
+    fold = 128 // total_rows
+    short = rows // fold
+    g_buf[me] = jnp.concatenate([gram[i * short : (i + 1) * short] for i in range(fold)], axis=1)
 
     @pl.loop(1, devices)
     def spread_gram(d):
         g_copy(lax.rem(me + d, devices), me).start()
+
+    relay_step(slab)
 
     @pl.loop(1, devices)
     def collect(d):
         other = lax.rem(me + d, devices)
         g_copy(other, other).wait_recv()
 
+    relay_step(slab + 1)
     blocks = []
     for s in range(tn):
         block = g_buf[s * pn]
         for q in range(1, pn):
             block = block + g_buf[s * pn + q]
-        blocks.append(block)
+        blocks += [block[:, i * total_rows : (i + 1) * total_rows] for i in range(fold)]
     square = jnp.concatenate(blocks, axis=0)
+    square = jnp.concatenate(
+        [square, jnp.zeros((total_rows, width - total_rows), jnp.float32)], axis=1
+    )
     padded = jnp.concatenate([square, jnp.zeros((width - total_rows, width), jnp.float32)], axis=0)
     symmetric = 0.5 * (square + jnp.transpose(padded)[:total_rows])
     row_of = lax.broadcasted_iota(jnp.int32, (total_rows, width), 0)
@@ -296,23 +368,21 @@
     keeping = (row_of < retained_ref[0]).astype(jnp.float32)
     inv_ref[...] = work * (1.0 / jnp.sqrt(pivots)) * keeping
     mine = inv_ref[pl.ds(pl.multiple_of(t * rows, rows), rows), :][:, total_rows : 2 * total_rows]
-    for d in range(1, tn):
-        s = lax.rem(t + d, tn)
-        for r in range(slab):
-            a_copy(s, s, r).wait_recv()
+    for e in range(slab + 2, slab + tn):
+        relay_step(e)
     for x in range(slab):
         every = jnp.concatenate([a_buf[s, x] for s in range(tn)], axis=0)
         out_ref[:, x, :] = jnp.dot(
             mine, every, precision=HIGHEST, preferred_element_type=jnp.float32
         )
 
-    for d in range(1, pn):
-        for r in range(slab):
-            rs_copy(lax.rem(p + d, pn), p, r).wait_send()
-    for d in range(1, tn):
-        t_copy(lax.rem(t + d, tn), t).wait_send()
-        for r in range(slab):
-            a_copy(lax.rem(t + d, tn), t, r).wait_send()
+    relayed(t_copy)
+    for r in range(slab):
+        for c in range(chips):
+            pair_copy(2 * c + 1 - core, r).wait_send()
+        for d in range(1, chips):
+            rs_copy(lax.rem(chip + d, chips), chip, r).wait_send()
+        relayed(a_copy, r)
 
     @pl.loop(1, devices)
     def drain(d):
@@ -361,14 +431,15 @@
             planes,
             pltpu.VMEM((length, length, rows, lanes), jnp.float32),
             planes,
-            pltpu.VMEM((pn, slab, rows, cells), jnp.float32),
+            pltpu.VMEM((pn // 2, slab, rows, cells), jnp.float32),
+            pltpu.VMEM((pn // 2, slab, rows, cells), jnp.float32),
             block,
             block,
             pltpu.VMEM((rows, total_rows), jnp.float32),
-            pltpu.VMEM((tn * pn, rows, width), jnp.float32),
+            pltpu.VMEM((tn * pn, rows * total_rows // 128, 128), jnp.float32),
             pltpu.VMEM((total_rows, width), jnp.float32),
-            dma((rows,)), dma((pn, slab)), dma((pn, slab)), dma((tn,)), dma((tn,)),
-            dma((tn, slab)), dma((tn, slab)), dma((tn * pn,)), dma((tn * pn,)),
+            dma((rows,)), dma((pn // 2, slab)), dma((pn // 2, slab)), dma((pn // 2, slab)),
+            dma((pn // 2, slab)), dma((2, tn)), dma((tn,)), dma((2, tn, slab)), dma((tn, slab)), dma((tn * pn,)), dma((tn * pn,)),
         ],
         compiler_params=pltpu.CompilerParams(collective_id=0, has_side_effects=True),
         name="exchange",

time: 47.7 us -> 46.7 us (0.979)
  Pallas kernels: 44.7 us -> 43.6 us
    pallas_call x1, Pallas kernels: 44.7 us -> 43.6 us  [shards(): pl.pallas_call(functools.partial(kernel, tn, pn), out_shape=jax.ShapeDtyp...]
where the time goes in v3:
time: 46.7 us; the launch traced here: 46.5 us
  Pallas kernels  43.6 us (93%)
  local copies, waits for them, and re-layouts  1.57 us (3%)
  between operations  1.3 us (3%)
    pallas_call x1, Pallas kernels, shards(): pl.pallas_call(functools.partial(kernel, tn, pn), out_shape=jax.ShapeDtyp...  43.6 us
    unnamed x1, local copies, waits for them, and re-layouts  1.57 us

profile of v3, /device:TPU:0, one launch (start us, length us, event | category | flops | bytes accessed | tf_op | source)
XLA Modules:
  0.0 46.5 jit_solution(12812344764243306299)
XLA Ops:
  1.3 43.6 %exchange.1 = f32[8,4,1024]{2,1,0:T(4,128)} custom-call(f32[8,32,1024]{2,1,0:T(8,128)} %t_hbm.1, f32[32,32,128]{2,1,0:T(8,128)} %psi_ref.1, bf16[256,256]{1,0:T(8,128)(2,1)} %constant.4.clone.weights_ref, f32[32,17,128]{2,1,0:T(8,128)} %constant.5.clone.table_ref, s32[1]{0:T(128)S(6)} %copy.8.occupied_ref, s32[1]{0:T(128)S(6)} %copy.9.retained_ref), custom_call_target="tpu_custom_call" | custom-call | tf_op jit(solution)/shard_map/exchange/pallas_call | solution.py:425
  45.0 1.6 %copy.10 = f32[8,4,1024]{2,1,0:T(4,128)} copy(f32[8,4,1024]{2,1,0:T(4,128)} %exchange.1) | data formatting | bytes 262144

commit v4 on v3

--- a/solution.py
+++ b/solution.py
@@ -139,10 +139,11 @@
             device_id=(t, q), device_id_type=MESH,
         )
 
-    def t_copy(s, side):
+    def t_copy(s, side, h):
+        piece = pl.ds(h * (slab // 2), slab // 2)
         return pltpu.make_async_remote_copy(
-            src_ref=t_buf.at[s], dst_ref=t_buf.at[s],
-            send_sem=t_send.at[(side + 1) // 2, s], recv_sem=t_recv.at[s],
+            src_ref=t_buf.at[s, piece], dst_ref=t_buf.at[s, piece],
+            send_sem=t_send.at[(side + 1) // 2, s, h], recv_sem=t_recv.at[s, h],
             device_id=(t + side, p), device_id_type=MESH,
         )
 
@@ -186,7 +187,8 @@
         )
 
     t_buf[t] = planes[pl.ds(p * slab, slab)]
-    relay(t_copy, 1)
+    relay(t_copy, 1, 0)
+    relay(t_copy, 1, 1)
 
     group_of = lax.broadcasted_iota(jnp.int32, (rows, lanes), 1) // length
     at_group = [group_of == g for g in range(groups)]
@@ -210,6 +212,10 @@
 
     @pl.loop(0, length // FORWARD)
     def forward(i):
+        @pl.when(i == 3 * length // (4 * FORWARD))
+        def second_hop():
+            relay(t_copy, 2, 0)
+
         density = []
         for j in range(FORWARD):
             x = i * FORWARD + j
@@ -227,10 +233,14 @@
             for m in range(length):
                 spec[i * FORWARD + j, m] = modes[m]
 
-    relay(t_copy, 2)
+    relay(t_copy, 2, 1)
 
     @pl.loop(0, length)
     def middle(m):
+        @pl.when(m == length // 2)
+        def third_hop():
+            relay(t_copy, 3, 0)
+
         modes = flat_dft([spec[x, m] for x in range(length)])
         half = length // 2
         scaled = []
@@ -242,7 +252,7 @@
             spec[x, m] = values[x]
 
     gram_ref[...] = jnp.zeros_like(gram_ref)
-    relay(t_copy, 3)
+    relay(t_copy, 3, 1)
 
     def relay_step(e):
         for hop in range(2, tn + 1):
@@ -316,10 +326,11 @@
                         part[x] = part[x] + pair_buf[owner // 2, r]
                         rs_copy(owner // 2, chip, r).start()
 
-        @pl.when(r == 0)
+        @pl.when(r == 1)
         def targets_in():
             for hop in range(4, tn + 1):
-                relay(t_copy, hop)
+                relay(t_copy, hop, 0)
+                relay(t_copy, hop, 1)
 
         @pl.when(r > 0)
         def earlier():
@@ -376,7 +387,8 @@
             mine, every, precision=HIGHEST, preferred_element_type=jnp.float32
         )
 
-    relayed(t_copy)
+    relayed(t_copy, 0)
+    relayed(t_copy, 1)
     for r in range(slab):
         for c in range(chips):
             pair_copy(2 * c + 1 - core, r).wait_send()
@@ -439,7 +451,7 @@
             pltpu.VMEM((tn * pn, rows * total_rows // 128, 128), jnp.float32),
             pltpu.VMEM((total_rows, width), jnp.float32),
             dma((rows,)), dma((pn // 2, slab)), dma((pn // 2, slab)), dma((pn // 2, slab)),
-            dma((pn // 2, slab)), dma((2, tn)), dma((tn,)), dma((2, tn, slab)), dma((tn, slab)), dma((tn * pn,)), dma((tn * pn,)),
+            dma((pn // 2, slab)), dma((2, tn, 2)), dma((tn, 2)), dma((2, tn, slab)), dma((tn, slab)), dma((tn * pn,)), dma((tn * pn,)),
         ],
         compiler_params=pltpu.CompilerParams(collective_id=0, has_side_effects=True),
         name="exchange",

time: 46.7 us -> 45.7 us (0.979)
  Pallas kernels: 43.6 us -> 42.7 us
    pallas_call x1, Pallas kernels: 43.6 us -> 42.7 us  [shards(): pl.pallas_call(functools.partial(kernel, tn, pn), out_shape=jax.ShapeDtyp...]
where the time goes in v4:
time: 45.7 us; the launch traced here: 45.6 us
  Pallas kernels  42.7 us (93%)
  local copies, waits for them, and re-layouts  1.57 us (3%)
  between operations  1.3 us (3%)
    pallas_call x1, Pallas kernels, shards(): pl.pallas_call(functools.partial(kernel, tn, pn), out_shape=jax.ShapeDtyp...  42.7 us
    unnamed x1, local copies, waits for them, and re-layouts  1.57 us

profile of v4, /device:TPU:0, one launch (start us, length us, event | category | flops | bytes accessed | tf_op | source)
XLA Modules:
  0.0 45.6 jit_solution(4130333241262309164)
XLA Ops:
  1.3 42.7 %exchange.1 = f32[8,4,1024]{2,1,0:T(4,128)} custom-call(f32[8,32,1024]{2,1,0:T(8,128)} %t_hbm.1, f32[32,32,128]{2,1,0:T(8,128)} %psi_ref.1, bf16[256,256]{1,0:T(8,128)(2,1)} %constant.4.clone.weights_ref, f32[32,17,128]{2,1,0:T(8,128)} %constant.5.clone.table_ref, s32[1]{0:T(128)S(6)} %copy.8.occupied_ref, s32[1]{0:T(128)S(6)} %copy.9.retained_ref), custom_call_target="tpu_custom_call" | custom-call | tf_op jit(solution)/shard_map/exchange/pallas_call | solution.py:437
  44.0 1.6 %copy.10 = f32[8,4,1024]{2,1,0:T(4,128)} copy(f32[8,4,1024]{2,1,0:T(4,128)} %exchange.1) | data formatting | bytes 262144

commit v5 on v4

--- a/solution.py
+++ b/solution.py
@@ -256,7 +256,7 @@
 
     def relay_step(e):
         for hop in range(2, tn + 1):
-            r = e - hop + 1
+            r = e - 2 * (hop - 1)
             if isinstance(e, int):
                 if 0 <= r < slab:
                     relay(a_copy, hop, r)
@@ -275,9 +275,11 @@
         a_buf[t, r] = own
         relay(a_copy, 1, r)
         relay_step(r)
+
+    def add_gram(r):
         every = jnp.concatenate([t_buf[s, r] for s in range(tn)], axis=0)
         gram_ref[...] += lax.dot_general(
-            own, every, (((1,), (1,)), ((), ())),
+            a_buf[t, r], every, (((1,), (1,)), ((), ())),
             precision=HIGHEST, preferred_element_type=jnp.float32,
         )
 
@@ -326,17 +328,18 @@
                         part[x] = part[x] + pair_buf[owner // 2, r]
                         rs_copy(owner // 2, chip, r).start()
 
-        @pl.when(r == 1)
-        def targets_in():
-            for hop in range(4, tn + 1):
-                relay(t_copy, hop, 0)
-                relay(t_copy, hop, 1)
-
-        @pl.when(r > 0)
+        @pl.when(r > 1)
         def earlier():
-            reduce_round(r - 1)
-
-    reduce_round(slab - 1)
+            reduce_round(r - 2)
+
+    for hop in range(4, tn + 1):
+        relay(t_copy, hop, 0)
+        relay(t_copy, hop, 1)
+    for r in range(slab - 2):
+        add_gram(r)
+    for r in range(slab - 2, slab):
+        reduce_round(r)
+        add_gram(r)
 
     gram = gram_ref[...] * (1.0 / all_cells)
     fold = 128 // total_rows
@@ -348,13 +351,15 @@
         g_copy(lax.rem(me + d, devices), me).start()
 
     relay_step(slab)
+    relay_step(slab + 1)
 
     @pl.loop(1, devices)
     def collect(d):
         other = lax.rem(me + d, devices)
         g_copy(other, other).wait_recv()
 
-    relay_step(slab + 1)
+    relay_step(slab + 2)
+    relay_step(slab + 3)
     blocks = []
     for s in range(tn):
         block = g_buf[s * pn]
@@ -379,7 +384,7 @@
     keeping = (row_of < retained_ref[0]).astype(jnp.float32)
     inv_ref[...] = work * (1.0 / jnp.sqrt(pivots)) * keeping
     mine = inv_ref[pl.ds(pl.multiple_of(t * rows, rows), rows), :][:, total_rows : 2 * total_rows]
-    for e in range(slab + 2, slab + tn):
+    for e in range(slab + 4, slab + 2 * (tn - 1)):
         relay_step(e)
     for x in range(slab):
         every = jnp.concatenate([a_buf[s, x] for s in range(tn)], axis=0)

time: 45.7 us -> 43.7 us (0.956)
  Pallas kernels: 42.7 us -> 40.7 us
    pallas_call x1, Pallas kernels: 42.7 us -> 40.7 us  [shards(): pl.pallas_call(functools.partial(kernel, tn, pn), out_shape=jax.ShapeDtyp...]
where the time goes in v5:
time: 43.7 us; the launch traced here: 43.6 us
  Pallas kernels  40.7 us (93%)
  local copies, waits for them, and re-layouts  1.57 us (4%)
  between operations  1.3 us (3%)
    pallas_call x1, Pallas kernels, shards(): pl.pallas_call(functools.partial(kernel, tn, pn), out_shape=jax.ShapeDtyp...  40.7 us
    unnamed x1, local copies, waits for them, and re-layouts  1.57 us

profile of v5, /device:TPU:0, one launch (start us, length us, event | category | flops | bytes accessed | tf_op | source)
XLA Modules:
  0.0 43.6 jit_solution(13279975571868788306)
XLA Ops:
  1.3 40.7 %exchange.1 = f32[8,4,1024]{2,1,0:T(4,128)} custom-call(f32[8,32,1024]{2,1,0:T(8,128)} %t_hbm.1, f32[32,32,128]{2,1,0:T(8,128)} %psi_ref.1, bf16[256,256]{1,0:T(8,128)(2,1)} %constant.4.clone.weights_ref, f32[32,17,128]{2,1,0:T(8,128)} %constant.5.clone.table_ref, s32[1]{0:T(128)S(6)} %copy.8.occupied_ref, s32[1]{0:T(128)S(6)} %copy.9.retained_ref), custom_call_target="tpu_custom_call" | custom-call | tf_op jit(solution)/shard_map/exchange/pallas_call | solution.py:442
  42.0 1.6 %copy.10 = f32[8,4,1024]{2,1,0:T(4,128)} copy(f32[8,4,1024]{2,1,0:T(4,128)} %exchange.1) | data formatting | bytes 262144
